TPU v7x, 256 devices: a whole 4x4x8 slice. The times are simulated.
256 devices in a mesh: view: 32 (over y, z), brick: 8 (over x, core).
Axes of the slice: x: 4, y: 4, z: 8, core: 2. Of those that a mesh axis runs over, the one named last changes fastest.
Arguments:
- volume: float32 [16, 8, 32, 128], P('brick'), may hold values from -6 to 6
- offsets: float32 [32, 3], P('view'), may hold values from 0 to 1
- shifts: int32 [32, 2], P('view'), may hold values from 0 to 127
- order: int32 [32], P('view'), may hold values from 0 to 1
- cond: float32 [32, 8], P('view'), may hold values from -6 to 6
- w_in: float32 [16, 128], replicated, may hold values from -1.5 to 1.5
- w_mid: float32 [128, 128], replicated, may hold values from -0.5 to 0.5
- w_out: float32 [128, 4], replicated, may hold values from -0.5 to 0.5
- cot_image: float32 [32, 3, 32, 128], P('view', None, 'brick'), may hold values from -0.12 to 0.12
Outputs:
- image: float32 [32, 3, 32, 128], P('view', None, 'brick')
- grad_in: float32 [16, 128], replicated
- grad_mid: float32 [128, 128], replicated
- grad_out: float32 [128, 4], replicated
Inputs may be any that keep to these rules, and one draw needn't show every extreme that they name: `order`: 0 marches towards higher slice numbers, 1 towards lower ones.
All inputs are finite; a program needn't handle non-finite values.
Results may differ from a plain program's by a relative error of at most 0.0003.
Values sent between devices are 32-bit elements; how exact they have to be, the bound alone decides.
No kernel may reach another device: no remote copies, remote signals or barrier semaphores. Data moves between devices by JAX's collectives and lax.ppermute only.
A program may use at most 64 MiB of HBM per device.

v0:
```python
import jax
import jax.numpy as jnp
from jax import lax
from jax.sharding import Mesh
from jax.sharding import PartitionSpec as P

BRICK = ("brick_0", "brick_1")
VIEW = ("view_0", "view_1")


STEP_DEPTH = 0.15
precise = lax.Precision.HIGHEST


def shifted_2(block, axis, distance):
    devices = range(lax.axis_size(axis))
    route = [(i - distance, i) for i in devices if i - distance in devices]
    return lax.ppermute(block, axis, route)


def filled_up(lines, peers):
    spare = -len(lines) % peers
    return jnp.pad(lines, [(0, spare)] + [(0, 0)] * (lines.ndim - 1))


def from_everyone(array, axis):
    peers = lax.axis_size(axis)
    return lax.all_to_all(
        jnp.broadcast_to(array[None], (peers, *array.shape)), axis, 0, 0, tiled=True
    )


def laid_out(parts, dim):
    dims = list(parts.shape[1:])
    dims[dim] *= parts.shape[0]
    return jnp.moveaxis(parts, 0, dim).reshape(dims)


def whole_of(array, axes, dim):
    far, near = axes
    initial = from_everyone(array, far)
    parts = jnp.swapaxes(from_everyone(initial, near), 0, 1)
    return laid_out(parts.reshape(-1, *array.shape), dim)


def split_up(array, dim, peers):
    before, after = (array.shape[:dim], array.shape[dim + 1 :])
    return jnp.moveaxis(array.reshape(*before, peers, -1, *after), dim, 0)


def sum_at_owner(array, axis, dim):
    parts = split_up(array, dim, lax.axis_size(axis))
    arrived = lax.all_to_all(parts, axis, split_axis=0, concat_axis=0, tiled=True)
    return arrived.sum(axis=0)


def sum_by_axis(array, axes, dim):
    far, near = axes
    parts = split_up(array, dim, lax.axis_size(far))
    nearer = sum_at_owner(parts, near, dim + 1)
    arrived = lax.all_to_all(nearer, far, split_axis=0, concat_axis=0, tiled=True)
    return arrived.sum(axis=0)


def sum_by_parts(array, axes):
    padded = filled_up(array, lax.axis_size(axes[0]) * lax.axis_size(axes[1]))
    whole = whole_of(sum_by_axis(padded, axes, 0), axes, 0)
    return lax.slice_in_dim(whole, 0, len(array)).reshape(array.shape)


def packed_total(arrays, axis):
    ends = [0]
    for a in arrays:
        ends.append(ends[-1] + a.size)
    subtotal = sum_by_parts(jnp.concatenate([a.ravel() for a in arrays]), axis)
    return tuple((subtotal[b:e].reshape(a.shape) for a, b, e in zip(arrays, ends, ends[1:])))


def resample(padded, shift_view, fraction):
    depthwise = (1.0 - fraction[2]) * padded[:-1] + fraction[2] * padded[1:]
    shifted = jnp.roll(depthwise, -shift_view[0], 2)
    shifted = (1.0 - fraction[0]) * shifted + fraction[0] * jnp.roll(shifted, -1, 2)
    columns = jnp.roll(shifted, -shift_view[1], 3)
    return (1.0 - fraction[1]) * columns + fraction[1] * jnp.roll(columns, -1, 3)


def transfer(weights, density, condition):
    w_in, w_mid, w_out = weights
    spread = jnp.broadcast_to(condition[:, None], (condition.shape[0], density.shape[1]))
    features = jnp.concatenate([density, spread], 0)
    hidden = jax.nn.silu(jnp.einsum("io,in->on", w_in, features, precision=precise))
    hidden = jax.nn.silu(jnp.einsum("io,in->on", w_mid, hidden, precision=precise))
    result = jnp.einsum("io,in->on", w_out, hidden, precision=precise)
    return jnp.concatenate([jax.nn.softplus(result[:1]), jax.nn.sigmoid(result[1:])], 0)


def composite(emitted):
    optical = emitted[:, 0] * STEP_DEPTH
    optical_depth = jnp.cumsum(optical, 0)
    transmit = jnp.exp(optical - optical_depth)
    opacity = -jnp.expm1(-optical)
    colour = jnp.sum((transmit * opacity)[:, None] * emitted[:, 1:], 0)
    return (colour, jnp.exp(-optical_depth[-1]))


def per_device(volume, offsets, shifts, order, cond, w_in, w_mid, w_out, cot_image):
    weights = (w_in, w_mid, w_out)
    fraction = offsets[0]
    shift_view = shifts[0]
    facing = order[0]
    condition = cond[0]
    next_slab = shifted_2(volume[0], BRICK, -1)
    samples = resample(jnp.concatenate([volume, next_slab[None]], 0), shift_view, fraction)
    slices, channels, rows_all, cols_all = samples.shape
    ray_count = rows_all * cols_all
    block_len = min(8192, ray_count)
    per_slice = ray_count // block_len
    blocks = slices * per_slice
    pieces = (
        samples.reshape(slices, channels, per_slice, block_len)
        .transpose(0, 2, 1, 3)
        .reshape(blocks, channels, block_len)
    )
    emitted = lax.map(lambda segment: transfer(weights, segment, condition), pieces)
    emitted = (
        emitted.reshape(slices, per_slice, 4, block_len)
        .transpose(0, 2, 1, 3)
        .reshape(slices, 4, ray_count)
    )

    def local_part(values):
        return composite(jnp.where(facing == 1, values[::-1], values))

    (colour, transmit), pull_local = jax.vjp(local_part, emitted)
    bricks = lax.axis_size(BRICK)
    partial_img = jnp.concatenate([colour, transmit[None]], 0).reshape(1, 4, rows_all, cols_all)
    received = lax.all_to_all(partial_img, BRICK, split_axis=2, concat_axis=0, tiled=True)
    ordered = jnp.where(facing == 1, received[::-1], received)
    cotangent = cot_image[0]
    sum_colour = jnp.zeros_like(cotangent)
    sum_transmit = jnp.ones_like(cotangent[0])
    fronts = []
    for position in range(bricks):
        fronts.append(sum_transmit)
        sum_colour = sum_colour + sum_transmit[None] * ordered[position, :3]
        sum_transmit = sum_transmit * ordered[position, 3]
    behind_colour = jnp.zeros_like(cotangent)
    gradients = [None] * bricks
    for position in reversed(range(bricks)):
        grad_piece = cotangent * fronts[position][None]
        gradients[position] = jnp.concatenate(
            [grad_piece, jnp.sum(grad_piece * behind_colour, 0)[None]], 0
        )
        behind_colour = ordered[position, :3] + ordered[position, 3][None] * behind_colour
    stacked = jnp.stack(gradients, 0)
    stacked = jnp.where(facing == 1, stacked[::-1], stacked)
    returned = lax.all_to_all(stacked, BRICK, split_axis=0, concat_axis=2, tiled=True).reshape(
        4, ray_count
    )
    grad_colour = returned[:3]
    grad_transmit = returned[3]
    grad_emitted = pull_local((grad_colour, grad_transmit))[0]
    grad_pieces = (
        grad_emitted.reshape(slices, 4, per_slice, block_len)
        .transpose(0, 2, 1, 3)
        .reshape(blocks, 4, block_len)
    )

    def accumulate(summed, element):
        segment, cotangent_block = element
        _, pullback = jax.vjp(lambda params: transfer(params, segment, condition), weights)
        return (jax.tree.map(jnp.add, summed, pullback(cotangent_block)[0]), None)

    initial = jax.tree.map(jnp.zeros_like, weights)
    summed, _ = lax.scan(accumulate, initial, (pieces, grad_pieces))
    grad_in, grad_mid, grad_out = packed_total(
        (summed[0], summed[1], summed[2]), (("view_0", "view_1"), ("brick_0", "brick_1"))
    )
    return (sum_colour[None], grad_in, grad_mid, grad_out)


def solution(mesh):
    torus = Mesh(mesh.devices.reshape(4, 8, 4, 2), ("view_0", "view_1", "brick_0", "brick_1"))
    return jax.shard_map(
        per_device,
        mesh=torus,
        in_specs=(
            P(BRICK, None, None, None),
            P(VIEW, None),
            P(VIEW, None),
            P(VIEW),
            P(VIEW, None),
            P(),
            P(),
            P(),
            P(VIEW, None, BRICK, None),
        ),
        out_specs=(P(VIEW, None, BRICK, None), P(), P(), P()),
        check_vma=False,
    )
```

profile of v0, /device:TPU:1, one launch (start us, length us, event | category | flops | bytes accessed | tf_op | source)
XLA Modules:
  0.0 152.4 jit_solution(4079354722425747048)
XLA Ops:
  1.5 5.1 %collective-permute-start = (f32[8,32,128]{2,1,0:T(8,128)S(1)}, f32[8,32,128]{2,1,0:T(8,128)S(1)}, u32[]{:S(2)}, u32[]{:S(2)}) collective-permute-start(f32[8,32,128]{2,1,0:T(8,128)S(1)} %slice_bitcast_fusion), channel_id=1, source_target_pairs={{1,0},{2,1},{3,2},{4,3},{5,4},{6,5},{7,6},{9,8},{10,9},{11,10},{12... | collective-permute-start | bytes 393224 | tf_op jit(solution)/shard_map/ppermute | solution.py:18
  18.8 16.4 %while.27 = (s32[]{:T(128)}, f32[2,4,4096]{2,1,0:T(4,128)S(1)}, f32[2,8,4096]{2,1,0:T(8,128)S(1)}, f32[1,8]{1,0:T(1,128)S(1)}, f32[16,128]{1,0:T(8,128)S(1)}, /*index=5*/f32[128,128]{1,0:T(8,128)S(1)}, f32[128,4]{0,1:T(4,128)S(1)}) while((s32[]{:T(128)}, f32[2,4,4096]{2,1,0:T(4,128)S(1)}, f32[2,8,4096]{2,1,0:T(8,128)S(1)}, ...), condition=%wide.region_1.2_spmd.clone, body=%wide.region_0.1_spmd.sunk.clone | while | flops 935473152 | bytes 9201921 | solution.py:124
  18.9 3.5 %convolution_bitcast_fusion.22 = f32[128,4096]{0,1:T(8,128)S(1)} fusion(f32[16,128]{1,0:T(8,128)S(1)} %get-tuple-element.389, f32[8,4096]{1,0:T(8,128)S(1)} %dynamic-slice_bitcast_fusion.8, f32[16]{0:T(128)S(1)} %pad.23.clone.3), kind=kOutput, calls=%fused_computation.1.clone.1.clone | convolution fusion | flops 100728832 | bytes 2236480 | tf_op jit(solution)/shard_map/while/body/eval_jaxpr/io,in->on/dot_general | solution.py:91
  22.4 2.1 %convolution_bitcast_fusion.23 = f32[128,4096]{0,1:T(8,128)S(1)} fusion(f32[128,128]{1,0:T(8,128)S(1)} %get-tuple-element.390, f32[128,4096]{0,1:T(8,128)S(1)} %convolution_bitcast_fusion.22), kind=kOutput, calls=%fused_computation.clone.1.clone | convolution fusion | flops 807403520 | bytes 4259840 | tf_op jit(solution)/shard_map/while/body/eval_jaxpr/io,in->on/dot_general | solution.py:92
  24.5 2.3 %convolution_bitcast_fusion.24 = f32[4,4096]{1,0:T(4,128)S(1)} fusion(f32[128,4]{0,1:T(4,128)S(1)} %get-tuple-element.391, f32[128,4096]{0,1:T(8,128)S(1)} %convolution_bitcast_fusion.23), kind=kOutput, calls=%fused_computation.2.clone.1.clone | convolution fusion | flops 27262976 | bytes 2164736 | tf_op jit(solution)/shard_map/while/body/eval_jaxpr/io,in->on/dot_general | solution.py:93
  27.1 3.5 %convolution_bitcast_fusion.22 = f32[128,4096]{0,1:T(8,128)S(1)} fusion(f32[16,128]{1,0:T(8,128)S(1)} %get-tuple-element.389, f32[8,4096]{1,0:T(8,128)S(1)} %dynamic-slice_bitcast_fusion.8, f32[16]{0:T(128)S(1)} %pad.23.clone.3), kind=kOutput, calls=%fused_computation.1.clone.1.clone | convolution fusion | flops 100728832 | bytes 2236480 | tf_op jit(solution)/shard_map/while/body/eval_jaxpr/io,in->on/dot_general | solution.py:91
  32.7 2.3 %convolution_bitcast_fusion.24 = f32[4,4096]{1,0:T(4,128)S(1)} fusion(f32[128,4]{0,1:T(4,128)S(1)} %get-tuple-element.391, f32[128,4096]{0,1:T(8,128)S(1)} %convolution_bitcast_fusion.23), kind=kOutput, calls=%fused_computation.2.clone.1.clone | convolution fusion | flops 27262976 | bytes 2164736 | tf_op jit(solution)/shard_map/while/body/eval_jaxpr/io,in->on/dot_general | solution.py:93
  35.6 7.4 %all_to_all.58 = f32[1,4,32,128]{3,1,0,2:T(4,128)S(1)} all-to-all(f32[1,4,32,128]{3,1,0,2:T(4,128)S(1)} %pad_maximum_fusion.5), channel_id=1, replica_groups=mesh['view_0'=4,'view_1'=8,'brick_0'=4,'brick_1'=2] {'brick_0','brick_1'}, dimensions={2} | all-to-all | bytes 131072 | tf_op jit(solution)/shard_map/all_to_all | solution.py:137
  43.9 4.0 %all-to-all-start.1 = ((f32[8,4,4,128]{3,2,1,0:T(4,128)}), f32[8,4,4,128]{3,2,1,0:T(4,128)S(1)}, u32[]{:S(2)}, u32[]{:S(2)}) async-start(f32[8,4,4,128]{3,2,1,0:T(4,128)} %reverse_select_fusion.1), calls=%async_computation.1 | async-start | bytes 131072 | tf_op jit(solution)/shard_map/all_to_all | solution.py:157
  47.9 4.9 %all-to-all-done.1 = f32[8,4,4,128]{3,2,1,0:T(4,128)S(1)} async-done(((f32[8,4,4,128]{3,2,1,0:T(4,128)}), f32[8,4,4,128]{3,2,1,0:T(4,128)S(1)}, u32[]{:S(2)}, u32[]{:S(2)}) %all-to-all-start.1) | async-done | bytes 65568 | tf_op jit(solution)/shard_map/all_to_all | solution.py:157
  53.6 42.6 %while.28 = (s32[]{:T(128)}, f32[16,128]{1,0:T(8,128)S(1)}, f32[128,128]{1,0:T(8,128)S(1)}, f32[128,4]{0,1:T(4,128)S(1)}, f32[2,8,4096]{2,1,0:T(8,128)S(1)}, /*i...) while((s32[]{:T(128)}, f32[16,128]{1,0:T(8,128)S(1)}, ...), condition=%wide.region_15.16_spmd.clone.clone, body=%wide.region_14.15_spmd.clone.sunk.clone | while | flops 2710893568 | bytes 28475764 | solution.py:175
  53.9 3.5 %convolution_bitcast_fusion.25 = f32[128,4096]{0,1:T(8,128)S(1)} fusion(f32[16,128]{1,0:T(8,128)S(1)} %get-tuple-element.419, f32[8,4096]{1,0:T(8,128)S(1)} %dynamic-slice_bitcast_fusion.9, f32[16]{0:T(128)S(1)} %pad.25.clone.3), kind=kOutput, calls=%fused_computation.32.clone.1.clone | convolution fusion | flops 100728832 | bytes 2236480 | tf_op jit(solution)/shard_map/while/body/eval_jaxpr/jvp(io,in->on)/dot_general | solution.py:91
  59.5 2.3 %convolution_bitcast_fusion.27 = f32[4,4096]{1,0:T(4,128)S(1)} fusion(f32[128,4]{0,1:T(4,128)S(1)} %get-tuple-element.421, f32[128,4096]{0,1:T(8,128)S(1)} %convolution_bitcast_fusion.26), kind=kOutput, calls=%fused_computation.33.clone.1.clone | convolution fusion | flops 27262976 | bytes 2164736 | tf_op jit(solution)/shard_map/while/body/eval_jaxpr/jvp(io,in->on)/dot_general | solution.py:93
  63.6 3.7 %fusion.177 = f32[128,4096]{0,1:T(8,128)S(1)} fusion(f32[128,4096]{0,1:T(8,128)S(1)} %convolution_bitcast_fusion.26, f32[128,4]{0,1:T(4,128)S(1)} %get-tuple-element.421, f32[1,4096]{1,0:T(1,128)S(1)} %fusion.175, f32[3,4096]{1,0:T(4,128)S(1)} %fusion.176), kind=kOutput, calls=%fused_computation.37.clone.1.clone | convolution fusion | flops 29900800 | bytes 4261888 | tf_op jit(solution)/shard_map/while/body/eval_jaxpr/transpose(jvp(io,in->on))/dot_general | solution.py:93
  67.3 3.8 %convolution_add_fusion.6 = f32[128,128]{1,0:T(8,128)S(1)} fusion(f32[128,4096]{0,1:T(8,128)S(1)} %fusion.177, f32[128,4096]{0,1:T(8,128)S(1)} %convolution_bitcast_fusion.25, f32[128,128]{1,0:T(8,128)S(1)} %get-tuple-element.404, pred[]{:T(512)S(6)} %compare.11), kind=kOutput, calls=%fused_computation.47.clone.1.clone | convolution fusion | flops 807436288 | bytes 4325377 | tf_op jit(solution)/shard_map/while/body/eval_jaxpr/transpose(jvp(io,in->on))/dot_general | solution.py:92
  75.0 3.5 %convolution_bitcast_fusion.25 = f32[128,4096]{0,1:T(8,128)S(1)} fusion(f32[16,128]{1,0:T(8,128)S(1)} %get-tuple-element.419, f32[8,4096]{1,0:T(8,128)S(1)} %dynamic-slice_bitcast_fusion.9, f32[16]{0:T(128)S(1)} %pad.25.clone.3), kind=kOutput, calls=%fused_computation.32.clone.1.clone | convolution fusion | flops 100728832 | bytes 2236480 | tf_op jit(solution)/shard_map/while/body/eval_jaxpr/jvp(io,in->on)/dot_general | solution.py:91
  80.6 2.3 %convolution_bitcast_fusion.27 = f32[4,4096]{1,0:T(4,128)S(1)} fusion(f32[128,4]{0,1:T(4,128)S(1)} %get-tuple-element.421, f32[128,4096]{0,1:T(8,128)S(1)} %convolution_bitcast_fusion.26), kind=kOutput, calls=%fused_computation.33.clone.1.clone | convolution fusion | flops 27262976 | bytes 2164736 | tf_op jit(solution)/shard_map/while/body/eval_jaxpr/jvp(io,in->on)/dot_general | solution.py:93
  84.7 3.7 %fusion.177 = f32[128,4096]{0,1:T(8,128)S(1)} fusion(f32[128,4096]{0,1:T(8,128)S(1)} %convolution_bitcast_fusion.26, f32[128,4]{0,1:T(4,128)S(1)} %get-tuple-element.421, f32[1,4096]{1,0:T(1,128)S(1)} %fusion.175, f32[3,4096]{1,0:T(4,128)S(1)} %fusion.176), kind=kOutput, calls=%fused_computation.37.clone.1.clone | convolution fusion | flops 29900800 | bytes 4261888 | tf_op jit(solution)/shard_map/while/body/eval_jaxpr/transpose(jvp(io,in->on))/dot_general | solution.py:93
  88.4 3.8 %convolution_add_fusion.6 = f32[128,128]{1,0:T(8,128)S(1)} fusion(f32[128,4096]{0,1:T(8,128)S(1)} %fusion.177, f32[128,4096]{0,1:T(8,128)S(1)} %convolution_bitcast_fusion.25, f32[128,128]{1,0:T(8,128)S(1)} %get-tuple-element.404, pred[]{:T(512)S(6)} %compare.11), kind=kOutput, calls=%fused_computation.47.clone.1.clone | convolution fusion | flops 807436288 | bytes 4325377 | tf_op jit(solution)/shard_map/while/body/eval_jaxpr/transpose(jvp(io,in->on))/dot_general | solution.py:92
  96.7 8.4 %all_to_all.59 = f32[8,32,74]{2,1,0:T(8,128)S(1)} all-to-all(f32[8,32,74]{2,1,0:T(8,128)S(1)} %copy.85), channel_id=1, replica_groups=mesh['view_0'=4,'view_1'=8,'brick_0'=4,'brick_1'=2] {'brick_0','brick_1'}, dimensions={0} | all-to-all | bytes 151552 | tf_op jit(solution)/shard_map/all_to_all | solution.py:53
  105.1 19.7 %all_to_all.60 = f32[32,1,74]{2,1,0:T(1,128)S(1)} all-to-all(f32[32,1,74]{2,1,0:T(1,128)S(1)} %bitcast.385), channel_id=1, replica_groups=mesh['view_0'=4,'view_1'=8,'brick_0'=4,'brick_1'=2] {'view_0','view_1'}, dimensions={0} | all-to-all | bytes 18944 | tf_op jit(solution)/shard_map/all_to_all | solution.py:61
  124.9 11.6 %all_to_all.61 = f32[32,1,74]{2,1,0:T(1,128)S(1)} all-to-all(f32[32,1,74]{2,1,0:T(1,128)S(1)} %broadcast_in_dim.114), channel_id=1, replica_groups=mesh['view_0'=4,'view_1'=8,'brick_0'=4,'brick_1'=2] {'view_0','view_1'}, dimensions={0} | all-to-all | bytes 18944 | tf_op jit(solution)/shard_map/all_to_all | solution.py:28
  137.1 6.7 %all-to-all-start.5 = ((f32[8,32,74]{2,1,0:T(8,128)}), f32[8,32,74]{2,1,0:T(8,128)S(1)}, u32[]{:S(2)}, u32[]{:S(2)}) async-start(f32[8,32,74]{2,1,0:T(8,128)} %broadcast_in_dim.116), calls=%async_computation.5 | async-start | bytes 262144 | tf_op jit(solution)/shard_map/all_to_all | solution.py:28
  144.5 4.7 %all-to-all-done.5 = f32[8,32,74]{2,1,0:T(8,128)S(1)} async-done(((f32[8,32,74]{2,1,0:T(8,128)}), f32[8,32,74]{2,1,0:T(8,128)S(1)}, u32[]{:S(2)}, u32[]{:S(2)}) %all-to-all-start.5) | async-done | bytes 75808 | tf_op jit(solution)/shard_map/all_to_all | solution.py:28
  (107 shorter events, 32.8 us)
Async XLA Ops:
  1.5 13.2 %collective-permute-start = (f32[8,32,128]{2,1,0:T(8,128)S(1)}, f32[8,32,128]{2,1,0:T(8,128)S(1)}, u32[]{:S(2)}, u32[]{:S(2)}) collective-permute-start(f32[8,32,128]{2,1,0:T(8,128)S(1)} %slice_bitcast_fusion), channel_id=1, source_target_pairs={{1,0},{2,1},{3,2},{4,3},{5,4},{6,5},{7,6},{9,8},{10,9},{11,10},{12... | collective-permute-start | bytes 393224 | tf_op jit(solution)/shard_map/ppermute | solution.py:18
  16.5 2.2 %copy-start = (f32[128,128]{1,0:T(8,128)S(1)}, f32[128,128]{1,0:T(8,128)}, u32[]{:S(2)}) copy-start(f32[128,128]{1,0:T(8,128)} %param.19) | copy-start | bytes 196612
  16.5 2.2 %copy-start.1 = (f32[16,128]{1,0:T(8,128)S(1)}, f32[16,128]{1,0:T(8,128)}, u32[]{:S(2)}) copy-start(f32[16,128]{1,0:T(8,128)} %param.18) | copy-start | bytes 24580
  16.5 2.2 %copy-start.3 = (f32[128,4]{0,1:T(4,128)S(1)}, f32[128,4]{0,1:T(4,128)}, u32[]{:S(2)}) copy-start(f32[128,4]{0,1:T(4,128)} %param.20) | copy-start | bytes 6148
  16.5 2.2 %copy-start.4 = (f32[1,8]{1,0:T(1,128)S(1)}, f32[1,8]{1,0:T(1,128)}, u32[]{:S(2)}) copy-start(f32[1,8]{1,0:T(1,128)} %param.17) | copy-start | bytes 100
  18.8 24.3 %copy-start.2 = (f32[1,3,4,128]{3,2,1,0:T(4,128)S(1)}, f32[1,3,4,128]{3,2,1,0:T(4,128)}, u32[]{:S(2)}) copy-start(f32[1,3,4,128]{3,2,1,0:T(4,128)} %param.21) | copy-start | bytes 18436
  43.9 8.9 %all-to-all-start.1 = ((f32[8,4,4,128]{3,2,1,0:T(4,128)}), f32[8,4,4,128]{3,2,1,0:T(4,128)S(1)}, u32[]{:S(2)}, u32[]{:S(2)}) async-start(f32[8,4,4,128]{3,2,1,0:T(4,128)} %reverse_select_fusion.1), calls=%async_computation.1 | async-start | bytes 131072 | tf_op jit(solution)/shard_map/all_to_all | solution.py:157
  137.1 12.0 %all-to-all-start.5 = ((f32[8,32,74]{2,1,0:T(8,128)}), f32[8,32,74]{2,1,0:T(8,128)S(1)}, u32[]{:S(2)}, u32[]{:S(2)}) async-start(f32[8,32,74]{2,1,0:T(8,128)} %broadcast_in_dim.116), calls=%async_computation.5 | async-start | bytes 262144 | tf_op jit(solution)/shard_map/all_to_all | solution.py:28
where the time goes:
time: 153 us; the launch traced here: 152 us
  matrix products  57.3 us (37%)
  blocking collectives  47.1 us (31%)
  starting transfers between devices  15.9 us (10%)
  waiting for transfers between devices  9.53 us (6%)
  local copies, waits for them, and re-layouts  8.74 us (6%)
  other arithmetic  6.97 us (5%)
  between operations  6.33 us (4%)
    dot_general x8, matrix products, transfer(): jnp.einsum('io,in->on', w_mid, hidden, precision=precise)  19.8 us
    dot_general x8, matrix products, transfer(): result = jnp.einsum('io,in->on', w_out, hidden, precision=precise)  19.7 us
    all_to_all x1, blocking collectives, sum_by_axis(): lax.all_to_all(nearer, far, split_axis=0, concat_axis=0, tiled=True)  19.7 us
    dot_general x6, matrix products, transfer(): jnp.einsum('io,in->on', w_in, features, precision=precise)  17.7 us
    all_to_all x1, blocking collectives, from_everyone(): lax.all_to_all(jnp.broadcast_to(array[None], (peers, *array.shape)), axis...  11.6 us
    all_to_all x1, blocking collectives, sum_at_owner(): lax.all_to_all(parts, axis, split_axis=0, concat_axis=0, tiled=True)  8.4 us
    all_to_all x1, blocking collectives, per_device(): lax.all_to_all(partial_img, BRICK, split_axis=2, concat_axis=0, tiled=True)  7.35 us
    all_to_all x1, starting transfers between devices, from_everyone(): lax.all_to_all(jnp.broadcast_to(array[None], (peers, *array.shape)), axis...  6.72 us
  transfers between devices with their start and end apart: 3, of which 2 were waited for; matrix products, arithmetic and copies ran while one was open for 2% of the time, Pallas kernels for 0%

commit v1 on v0

v1 whole, which is shorter than its diff:
```python
import functools

import jax
import jax.numpy as jnp
from jax import lax
from jax.experimental import pallas as pl
from jax.experimental.pallas import tpu as pltpu
from jax.sharding import Mesh
from jax.sharding import PartitionSpec as P

VIEW = ("y_far", "y_near", "z")
BRICK = ("x", "core")
NEAR = ("y_near", "x", "core")
FAR = ("y_far", "z")

STEP_DEPTH = 0.15
NZ, CH, COND, HID = 16, 8, 8, 128
PX, PY = 32, 128
ROWS = 4
RAYS = ROWS * PY
PIECES, PIECE_ROWS = 16, 16
UNROLL = 2

bf16, f32 = jnp.bfloat16, jnp.float32
VMEM = pl.BlockSpec(memory_space=pltpu.VMEM)
SMEM = pl.BlockSpec(memory_space=pltpu.SMEM)


def split(value):
    high = value.astype(bf16)
    return high, (value - high.astype(f32)).astype(bf16)


def split3(value):
    high = value.astype(bf16).astype(f32)
    rest = value - high
    middle = rest.astype(bf16).astype(f32)
    return high, middle, rest - middle


def mul(a, b):
    return jnp.dot(a, b, preferred_element_type=f32)


def mul_t(a, b):
    return lax.dot_general(a, b, (((1,), (1,)), ((), ())), preferred_element_type=f32)


def two_halves(value):
    return value[: value.shape[0] // 2] + value[value.shape[0] // 2 :]


def two_sides(value):
    return value[:, : value.shape[1] // 2] + value[:, value.shape[1] // 2 :]


def get(ref, rows):
    return jnp.concatenate([ref[r, rows, :] for r in range(ROWS)], 1)


def put(ref, rows, value):
    for r in range(ROWS):
        ref[r, rows, :] = value[:, r * PY : (r + 1) * PY]


def resample_kernel(offsets, shifts, volume, out):
    f_row, f_col = offsets[0, 0], offsets[0, 1]
    row_shift = shifts[0, 0] & (PX - 1)
    col_shift = shifts[0, 1] & (PY - 1)
    roll_near = (PY - col_shift) & (PY - 1)
    roll_far = (PY - 1 - col_shift) & (PY - 1)

    for s in range(2):

        def source(i):
            row = (i + row_shift) & (PX - 1)
            return volume[pl.ds(s * CH * PX + row, CH, stride=PX), :]

        near = source(0)
        for i in range(PX):
            far = source(i + 1)
            row = (1.0 - f_row) * near + f_row * far
            near = far
            value = (1.0 - f_col) * pltpu.roll(row, roll_near, 1) + f_col * pltpu.roll(
                row, roll_far, 1
            )
            out[i // ROWS, s, i % ROWS] = value


def weights_kernel(cond, w_in, w_mid, w_out_t, lhs_in, lhs_mid, lhs_out, back_mid, back_out):
    half_in = 0.5 * w_in[...]
    high, low = split(half_in[:CH])
    high, low = high.astype(f32), low.astype(f32)
    bias = cond[0, 0] * half_in[CH : CH + 1]
    for c in range(1, COND):
        bias = bias + cond[0, c] * half_in[CH + c : CH + c + 1]
    rows = jnp.concatenate([high, high, low, *split3(bias), jnp.zeros((5, HID), f32)], 0)
    lhs_in[...] = rows.T.astype(bf16)

    half_mid = 0.5 * w_mid[...]
    high, low = split(half_mid.T)
    lhs_mid[:HID, :HID] = high
    lhs_mid[:HID, HID:] = high
    lhs_mid[HID:, :HID] = low
    lhs_mid[HID:, HID:] = low
    high, low = split(half_mid)
    back_mid[:HID, :HID] = high
    back_mid[:HID, HID:] = high
    back_mid[HID:, :HID] = low
    back_mid[HID:, HID:] = low

    out_t = w_out_t[...]
    high, low = split(out_t)
    high, low = high.astype(f32), low.astype(f32)
    pair = jnp.concatenate([high, low, jnp.zeros((8, HID), f32)], 0).astype(bf16)
    lhs_out[:, :HID] = pair
    lhs_out[:, HID:] = pair
    rows = 0.5 * jnp.concatenate([high, high, low, jnp.zeros((4, HID), f32)], 0)
    back_out[...] = rows.T.astype(bf16)


def activate(half):
    t = jnp.tanh(half)
    up = 1.0 + t
    value = half * up
    return value, up + value * (1.0 - t)


def softplus(x):
    z = jnp.exp(-jnp.abs(x))
    series = z * (1.0 - z * (0.5 - z * (1.0 / 3.0 - z * 0.25)))
    return jnp.maximum(x, 0.0) + jnp.where(z < 0.03, series, jnp.log(1.0 + z))


def one_minus_exp(x):
    terms = (1.0 / 2, 1.0 / 3, 1.0 / 4, 1.0 / 5, 1.0 / 6, 1.0 / 7)
    series = jnp.ones_like(x)
    for factor in reversed(terms):
        series = 1.0 - x * factor * series
    return jnp.where(x < 0.25, x * series, 1.0 - jnp.exp(-x))


def logistic(x):
    return 1.0 / (1.0 + jnp.exp(-x))


def render_kernel(
    offsets,
    order,
    cond,
    slices,
    cot,
    lhs_in,
    lhs_mid,
    lhs_out,
    back_mid,
    back_out,
    image,
    grads,
    feats,
    h1,
    d1,
    h2,
    d2,
    raw,
    graw,
    acc_mid,
    acc_in,
    acc_out,
):
    f_depth = offsets[0, 2]
    facing = order[0]

    def forward(k):
        f_next = jnp.where(k == NZ - 1, 0.0, f_depth)
        after = jnp.minimum(k + 1, NZ - 1)
        x = jnp.concatenate(
            [(1.0 - f_depth) * slices[k, r] + f_next * slices[after, r] for r in range(ROWS)], 1
        )
        high = x.astype(bf16).astype(f32)
        features = jnp.concatenate([high, x - high, high, jnp.ones_like(x)], 0).astype(bf16)
        feats[k] = features
        value, slope = activate(mul(lhs_in[...], features))
        high, low = split(value)
        d1[k] = slope
        h1[k, :HID] = high
        h1[k, HID:] = low
        pair = jnp.concatenate([high, low], 0)
        value, slope = activate(two_halves(mul(lhs_mid[...], pair)))
        high, low = split(value)
        d2[k] = slope
        h2[k, :HID] = high
        h2[k, HID:] = low
        pair = jnp.concatenate([high, low], 0)
        result = mul(lhs_out[...], pair)[:8]
        put(raw, pl.ds(pl.multiple_of(8 * k, 8), 8), result + pltpu.roll(result, 4, 0))

    def forward_some(i, carry):
        for u in range(UNROLL):
            forward(i * UNROLL + u)
        return carry

    lax.fori_loop(0, NZ // UNROLL, forward_some, 0)

    def strided(ref, o):
        return get(ref, pl.ds(o, NZ, stride=8))

    row = lax.broadcasted_iota(jnp.int32, (NZ, NZ), 0)
    column = lax.broadcasted_iota(jnp.int32, (NZ, NZ), 1)
    sign = 1 - 2 * facing
    earlier = jnp.where((row - column) * sign > 0, 1.0, 0.0)
    later = jnp.where((column - row) * sign > 0, 1.0, 0.0)

    def summed(mask, value):
        mask = jnp.concatenate([mask] * 3, 1).astype(bf16)
        return mul(mask, jnp.concatenate(split3(value), 0).astype(bf16))

    raw_sigma = strided(raw, 0)
    optical = STEP_DEPTH * softplus(raw_sigma)
    transmit = jnp.exp(-summed(earlier, optical))
    weight = transmit * one_minus_exp(optical)
    gain = jnp.zeros_like(weight)
    for c in range(3):
        rgb = logistic(strided(raw, c + 1))
        picture = jnp.sum(weight * rgb, 0, keepdims=True)
        for r in range(ROWS):
            image[c, r : r + 1, :] = picture[:, r * PY : (r + 1) * PY]
        cot_c = jnp.concatenate([cot[c, r : r + 1, :] for r in range(ROWS)], 1)
        gain = gain + cot_c * rgb
        put(graw, pl.ds(c + 1, NZ, stride=8), weight * cot_c * (rgb * (1.0 - rgb)))
    grad_optical = gain * transmit * jnp.exp(-optical) - summed(later, gain * weight)
    put(graw, pl.ds(0, NZ, stride=8), STEP_DEPTH * grad_optical * logistic(raw_sigma))

    acc_mid[...] = jnp.zeros_like(acc_mid)
    acc_in[...] = jnp.zeros_like(acc_in)
    acc_out[...] = jnp.zeros_like(acc_out)
    first = lax.broadcasted_iota(jnp.int32, (8, RAYS), 0) < 4

    def backward(k):
        g = get(graw, pl.ds(pl.multiple_of(8 * k, 8), 8))
        g = jnp.where(first, g, pltpu.roll(g, 4, 0))
        high = g.astype(bf16).astype(f32)
        pair = jnp.where(first, high, g - high)
        cotangent = jnp.concatenate([pair, jnp.where(first, high, 0.0)], 0).astype(bf16)
        delta = mul(back_out[...], cotangent) * d2[k]
        acc_out[...] += mul_t(cotangent, h2[k])
        pair = jnp.concatenate(split(delta), 0)
        acc_mid[...] += mul_t(h1[k], pair)
        delta = two_halves(mul(back_mid[...], pair)) * d1[k]
        pair = jnp.concatenate(split(delta), 0)
        acc_in[...] += mul_t(feats[k], pair)

    def backward_some(i, carry):
        for u in range(UNROLL):
            backward(i * UNROLL + u)
        return carry

    lax.fori_loop(0, NZ // UNROLL, backward_some, 0)

    grads[:HID] = two_sides(two_halves(acc_mid[...]))
    total = two_sides(acc_in[...])
    grads[HID : HID + CH] = total[:CH] + total[CH : 2 * CH]
    for c in range(COND):
        grads[HID + CH + c : HID + CH + c + 1] = cond[0, c] * total[3 * CH : 3 * CH + 1]
    total = two_sides(acc_out[...])[:8]
    used = HID + CH + COND
    grads[used : used + 8] = total + pltpu.roll(total, 4, 0)
    grads[used + 8 :] = jnp.zeros((grads.shape[0] - used - 8, HID), f32)


def sum_kernel(parts, out):
    total = parts[0]
    for i in range(1, PIECES):
        total = total + parts[i]
    for i in range(PIECES):
        out[i] = total


def unpack_kernel(packed, grad_in, grad_mid, grad_out_t):
    grad_mid[...] = packed[:HID]
    grad_in[...] = packed[HID : HID + CH + COND]
    grad_out_t[...] = packed[HID + CH + COND : HID + CH + COND + 4]


def shape(dims, dtype=f32):
    return jax.ShapeDtypeStruct(dims, dtype)


def exchange(parts, axes):
    return lax.all_to_all(parts, axes, 0, 0, tiled=True)


def per_device(volume, offsets, shifts, order, cond, w_in, w_mid, w_out, cot_image):
    rows = pl.pallas_call(
        resample_kernel,
        out_shape=shape((8, 2, ROWS, CH, PY)),
        in_specs=[SMEM, SMEM, VMEM],
        out_specs=VMEM,
    )(offsets, shifts, volume.reshape(2 * CH * PX, PY))
    slices = exchange(rows, BRICK).reshape(NZ, ROWS, CH, PY)
    weights = pl.pallas_call(
        weights_kernel,
        out_shape=(
            shape((HID, 32), bf16),
            shape((2 * HID, 2 * HID), bf16),
            shape((16, 2 * HID), bf16),
            shape((2 * HID, 2 * HID), bf16),
            shape((HID, 16), bf16),
        ),
        in_specs=[SMEM, VMEM, VMEM, VMEM],
        out_specs=(VMEM,) * 5,
    )(cond, w_in, w_mid, w_out.T)
    image, grads = pl.pallas_call(
        render_kernel,
        out_shape=(shape((3, ROWS, PY)), shape((PIECES * PIECE_ROWS, HID))),
        in_specs=[SMEM, SMEM, SMEM] + [VMEM] * 7,
        out_specs=(VMEM, VMEM),
        scratch_shapes=[
            pltpu.VMEM((NZ, 32, RAYS), bf16),
            pltpu.VMEM((NZ, 2 * HID, RAYS), bf16),
            pltpu.VMEM((NZ, HID, RAYS), f32),
            pltpu.VMEM((NZ, 2 * HID, RAYS), bf16),
            pltpu.VMEM((NZ, HID, RAYS), f32),
            pltpu.VMEM((ROWS, NZ * 8, PY), f32),
            pltpu.VMEM((ROWS, NZ * 8, PY), f32),
            pltpu.VMEM((2 * HID, 2 * HID), f32),
            pltpu.VMEM((32, 2 * HID), f32),
            pltpu.VMEM((16, 2 * HID), f32),
        ],
    )(offsets, order, cond, slices, cot_image[0], *weights)

    def total(parts):
        return pl.pallas_call(
            sum_kernel, out_shape=shape(parts.shape), in_specs=[VMEM], out_specs=VMEM
        )(parts)

    parts = grads.reshape(PIECES, PIECE_ROWS, HID)
    parts = total(exchange(parts, NEAR))
    parts = total(exchange(parts, FAR))
    packed = exchange(parts, NEAR).reshape(PIECES * PIECE_ROWS, HID)
    grad_in, grad_mid, grad_out_t = pl.pallas_call(
        unpack_kernel,
        out_shape=(shape((CH + COND, HID)), shape((HID, HID)), shape((4, HID))),
        in_specs=[VMEM],
        out_specs=(VMEM,) * 3,
    )(packed)
    return image[None], grad_in, grad_mid, grad_out_t.T


def solution(mesh):
    torus = Mesh(
        mesh.devices.reshape(2, 2, 8, 4, 2), ("y_far", "y_near", "z", "x", "core")
    )
    return jax.shard_map(
        per_device,
        mesh=torus,
        in_specs=(
            P(BRICK, None, None, None),
            P(VIEW, None),
            P(VIEW, None),
            P(VIEW),
            P(VIEW, None),
            P(),
            P(),
            P(),
            P(VIEW, None, BRICK, None),
        ),
        out_specs=(P(VIEW, None, BRICK, None), P(), P(), P()),
        check_vma=False,
    )
```

time: 153 us -> 85.3 us (0.56)
  matrix products: 57.3 us -> 0 us
  Pallas kernels: 0 us -> 29.3 us
  starting transfers between devices: 15.9 us -> 6.51 us
  local copies, waits for them, and re-layouts: 8.74 us -> 0.7 us
  other arithmetic: 6.97 us -> 0 us
  waiting for transfers between devices: 9.53 us -> 4.22 us
  between operations: 6.33 us -> 1.29 us
  blocking collectives: 47.1 us -> 42.6 us
    dot_general x22 -> x0, matrix products: 57.3 us -> none  [the longest x8 19.8 us: transfer(): jnp.einsum('io,in->on', w_mid, hidden, precision=precise)]
    pallas_call x0 -> x6, Pallas kernels: none -> 29.3 us  [the longest x1 21 us: per_device(): pl.pallas_call(render_kernel, out_shape=(shape((3, ROWS, PY)), shape((PIE...]
    slice x14 -> x0, local copies, waits for them, and re-layouts: 5.53 us -> none  [the longest x5 2.57 us: packed_total(): subtotal[b:e].reshape(a.shape)]
    all_to_all x2 -> x1, waiting for transfers between devices: 9.52 us -> 4.22 us  [exchange(): return lax.all_to_all(parts, axes, 0, 0, tiled=True)]
    ppermute x1 -> x0, starting transfers between devices: 5.11 us -> none  [shifted_2(): return lax.ppermute(block, axis, route)]
    all_to_all x4 -> x3, blocking collectives: 47.1 us -> 42.6 us  [exchange(): return lax.all_to_all(parts, axes, 0, 0, tiled=True)]
    all_to_all x2 -> x1, starting transfers between devices: 10.7 us -> 6.51 us  [exchange(): return lax.all_to_all(parts, axes, 0, 0, tiled=True)]
    add x4 -> x0, other arithmetic: 4.01 us -> none  [the longest x1 1.67 us: resample(): depthwise = (1.0 - fraction[2]) * padded[:-1] + fraction[2] * padded[1:]]
  transfers between devices with their start and end apart: 3 -> 1, of which waited for: 2 -> 1; matrix products, arithmetic and copies ran while one was open for 2% -> 0% of each run, Pallas kernels for 0% -> 2%
where the time goes in v1:
time: 85.3 us; the launch traced here: 84.7 us
  blocking collectives  42.6 us (50%)
  Pallas kernels  29.3 us (34%)
  starting transfers between devices  6.51 us (8%)
  waiting for transfers between devices  4.22 us (5%)
  between operations  1.29 us (2%)
    all_to_all x3, blocking collectives, exchange(): return lax.all_to_all(parts, axes, 0, 0, tiled=True)  42.6 us
    pallas_call x1, Pallas kernels, per_device(): pl.pallas_call(render_kernel, out_shape=(shape((3, ROWS, PY)), shape((PIE...  21 us
    all_to_all x1, starting transfers between devices, exchange(): return lax.all_to_all(parts, axes, 0, 0, tiled=True)  6.51 us
    all_to_all x1, waiting for transfers between devices, exchange(): return lax.all_to_all(parts, axes, 0, 0, tiled=True)  4.22 us
    pallas_call x2, Pallas kernels, total(): pl.pallas_call(sum_kernel, out_shape=shape(parts.shape), in_specs=[VMEM],...  3.16 us
    pallas_call x1, Pallas kernels, per_device(): pl.pallas_call(resample_kernel, out_shape=shape((8, 2, ROWS, CH, PY)), in...  2.02 us
  transfers between devices with their start and end apart: 1, of which 1 were waited for; matrix products, arithmetic and copies ran while one was open for 0% of the time, Pallas kernels for 2%

profile of v1, /device:TPU:1, one launch (start us, length us, event | category | flops | bytes accessed | tf_op | source)
XLA Modules:
  0.0 84.7 jit_solution(16615228763696833730)
XLA Ops:
  0.6 2.0 %shard_map.120 = f32[8,2,4,8,128]{4,3,2,1,0:T(8,128)} custom-call(f32[1,3]{1,0:T(1,128)} %offsets.3, s32[1,2]{1,0:T(1,128)} %shifts.1, f32[512,128]{1,0:T(8,128)} %bitcast.10), custom_call_target="tpu_custom_call" | custom-call | tf_op jit(solution)/shard_map/pallas_call | solution.py:294
  2.6 6.5 %all-to-all-start = ((f32[8,2,4,8,128]{4,3,2,1,0:T(8,128)}), f32[8,2,4,8,128]{4,3,2,1,0:T(8,128)S(1)}, u32[]{:S(2)}, u32[]{:S(2)}) async-start(f32[8,2,4,8,128]{4,3,2,1,0:T(8,128)} %shard_map.120), calls=%async_computation | async-start | bytes 524288 | tf_op jit(solution)/shard_map/all_to_all | solution.py:290
  9.8 1.6 %shard_map.121 = (bf16[128,32]{1,0:T(8,128)(2,1)}, bf16[256,256]{1,0:T(8,128)(2,1)}, bf16[16,256]{1,0:T(8,128)(2,1)}, bf16[256,256]{1,0:T(8,128)(2,1)}, bf16[128,16]{1,0:T(8,128)(2,1)}) custom-call(f32[1,8]{1,0:T(1,128)} %cond.3, f32[16,128]{1,0:T(8,128)} %w_in.1, f32[128,128]{1,0:T(8,128)} %w_mid.1, f32[4,128]{1,0:T(4,128)} %bitcast.13), custom_call_target="tpu_custom_call" | custom-call | tf_op jit(solution)/shard_map/pallas_call | solution.py:301
  11.4 4.2 %all-to-all-done = f32[8,2,4,8,128]{4,3,2,1,0:T(8,128)S(1)} async-done(((f32[8,2,4,8,128]{4,3,2,1,0:T(8,128)}), f32[8,2,4,8,128]{4,3,2,1,0:T(8,128)S(1)}, u32[]{:S(2)}, u32[]{:S(2)}) %all-to-all-start) | async-done | bytes 262176 | tf_op jit(solution)/shard_map/all_to_all | solution.py:290
  15.7 0.0 copy-start
  15.7 0.7 copy-done
  16.4 21.0 %shard_map.122 = (f32[3,4,128]{2,1,0:T(4,128)}, f32[256,128]{1,0:T(8,128)}) custom-call(f32[1,3]{1,0:T(1,128)} %offsets.3, s32[1]{0:T(128)S(6)} %copy.13.order, f32[1,8]{1,0:T(1,128)} %cond.3, f32[16,4,8,128]{3,2,1,0:T(8,128)} %bitcast.8, f32[3,4,128]{2,1,0:T(4,128)} %bitcast.12, bf16[128,32]{1,0:T(8,128)(2,1)} %get-tuple-element.14.lhs_in, ...), custom_call_target="tpu_custom_call" | custom-call | tf_op jit(solution)/shard_map/pallas_call | solution.py:313
  37.4 11.2 %all_to_all.20.parts = f32[16,16,128]{2,1,0:T(8,128)} all-to-all(f32[16,16,128]{2,1,0:T(8,128)} %bitcast.11), channel_id=1, replica_groups=mesh['y_far'=2,'y_near'=2,'z'=8,'x'=4,'core'=2] {'y_near','x','core'}, dimensions={0} | all-to-all | bytes 262144 | tf_op jit(solution)/shard_map/all_to_all | solution.py:290
  48.5 1.6 %shard_map.123 = f32[16,16,128]{2,1,0:T(8,128)} custom-call(f32[16,16,128]{2,1,0:T(8,128)} %all_to_all.20.parts), custom_call_target="tpu_custom_call" | custom-call | tf_op jit(solution)/shard_map/pallas_call | solution.py:333
  50.1 19.2 %all_to_all.21.parts = f32[16,16,128]{2,1,0:T(8,128)} all-to-all(f32[16,16,128]{2,1,0:T(8,128)} %shard_map.123), channel_id=1, replica_groups=mesh['y_far'=2,'y_near'=2,'z'=8,'x'=4,'core'=2] {'y_far','z'}, dimensions={0} | all-to-all | bytes 262144 | tf_op jit(solution)/shard_map/all_to_all | solution.py:290
  69.3 1.6 %shard_map.124 = f32[16,16,128]{2,1,0:T(8,128)} custom-call(f32[16,16,128]{2,1,0:T(8,128)} %all_to_all.21.parts), custom_call_target="tpu_custom_call" | custom-call | tf_op jit(solution)/shard_map/pallas_call | solution.py:333
  70.9 12.2 %all_to_all.22 = f32[16,16,128]{2,1,0:T(8,128)} all-to-all(f32[16,16,128]{2,1,0:T(8,128)} %shard_map.124), channel_id=1, replica_groups=mesh['y_far'=2,'y_near'=2,'z'=8,'x'=4,'core'=2] {'y_near','x','core'}, dimensions={0} | all-to-all | bytes 262144 | tf_op jit(solution)/shard_map/all_to_all | solution.py:290
  83.2 1.5 %shard_map.125 = (f32[16,128]{1,0:T(8,128)}, f32[128,128]{1,0:T(8,128)}, f32[4,128]{1,0:T(4,128)}) custom-call(f32[256,128]{1,0:T(8,128)} %bitcast.9), custom_call_target="tpu_custom_call" | custom-call | tf_op jit(solution)/shard_map/pallas_call | solution.py:341
Async XLA Ops:
  2.6 13.0 %all-to-all-start = ((f32[8,2,4,8,128]{4,3,2,1,0:T(8,128)}), f32[8,2,4,8,128]{4,3,2,1,0:T(8,128)S(1)}, u32[]{:S(2)}, u32[]{:S(2)}) async-start(f32[8,2,4,8,128]{4,3,2,1,0:T(8,128)} %shard_map.120), calls=%async_computation | async-start | bytes 524288 | tf_op jit(solution)/shard_map/all_to_all | solution.py:290
  15.7 0.7 copy-start

commit v2 on v1

--- a/solution.py
+++ b/solution.py
@@ -19,7 +19,6 @@
 ROWS = 4
 RAYS = ROWS * PY
 PIECES, PIECE_ROWS = 16, 16
-UNROLL = 2
 
 bf16, f32 = jnp.bfloat16, jnp.float32
 VMEM = pl.BlockSpec(memory_space=pltpu.VMEM)
@@ -87,7 +86,9 @@
             out[i // ROWS, s, i % ROWS] = value
 
 
-def weights_kernel(cond, w_in, w_mid, w_out_t, lhs_in, lhs_mid, lhs_out, back_mid, back_out):
+def prepare_kernel(
+    offsets, order, cond, w_in, w_mid, w_out_t, cot_rows, per_ray, per_channel, masks, lhs_in, lhs_mid, lhs_out, back_mid, back_out
+):
     half_in = 0.5 * w_in[...]
     high, low = split(half_in[:CH])
     high, low = high.astype(f32), low.astype(f32)
@@ -118,12 +119,27 @@
     rows = 0.5 * jnp.concatenate([high, high, low, jnp.zeros((4, HID), f32)], 0)
     back_out[...] = rows.T.astype(bf16)
 
+    for c in range(3):
+        for r in range(ROWS):
+            per_ray[c : c + 1, r * PY : (r + 1) * PY] = cot_rows[c, r : r + 1, :]
+    per_ray[3:] = jnp.full((5, RAYS), offsets[0, 2], f32)
+    for c in range(COND):
+        per_channel[c : c + 1] = jnp.full((1, HID), cond[0, c], f32)
+
+    row = lax.broadcasted_iota(jnp.int32, (2 * NZ, 3 * NZ), 0)
+    column = lax.broadcasted_iota(jnp.int32, (2 * NZ, 3 * NZ), 1) & (NZ - 1)
+    ahead = ((row & (NZ - 1)) - column) * (1 - 2 * order[0])
+    ahead = jnp.where(row < NZ, ahead, -ahead)
+    masks[...] = jnp.where(ahead > 0, 1.0, 0.0).astype(bf16)
+
 
 def activate(half):
-    t = jnp.tanh(half)
-    up = 1.0 + t
-    value = half * up
-    return value, up + value * (1.0 - t)
+    up = 1.0 + jnp.tanh(half)
+    return half * up, up
+
+
+def slope_of(value, up):
+    return up + value * (2.0 - up)
 
 
 def softplus(x):
@@ -145,11 +161,10 @@
 
 
 def render_kernel(
-    offsets,
-    order,
-    cond,
     slices,
-    cot,
+    per_ray,
+    per_channel,
+    masks,
     lhs_in,
     lhs_mid,
     lhs_out,
@@ -157,21 +172,15 @@
     back_out,
     image,
     grads,
-    feats,
-    h1,
-    d1,
-    h2,
-    d2,
-    raw,
-    graw,
-    acc_mid,
-    acc_in,
-    acc_out,
+    *scratch,
 ):
-    f_depth = offsets[0, 2]
-    facing = order[0]
-
-    def forward(k):
+    raw, graw, acc_mid, acc_in, acc_out = scratch[-5:]
+    feats, h1, h2, value1, up1, value2, up2 = zip(scratch[:7], scratch[7:14])
+    delta2, delta1 = zip(scratch[14:16], scratch[16:18])
+
+    def layer_in(i, p):
+        k = 2 * i + p
+        f_depth = per_ray[3:4, :PY]
         f_next = jnp.where(k == NZ - 1, 0.0, f_depth)
         after = jnp.minimum(k + 1, NZ - 1)
         x = jnp.concatenate(
@@ -179,45 +188,34 @@
         )
         high = x.astype(bf16).astype(f32)
         features = jnp.concatenate([high, x - high, high, jnp.ones_like(x)], 0).astype(bf16)
-        feats[k] = features
-        value, slope = activate(mul(lhs_in[...], features))
-        high, low = split(value)
-        d1[k] = slope
-        h1[k, :HID] = high
-        h1[k, HID:] = low
-        pair = jnp.concatenate([high, low], 0)
-        value, slope = activate(two_halves(mul(lhs_mid[...], pair)))
-        high, low = split(value)
-        d2[k] = slope
-        h2[k, :HID] = high
-        h2[k, HID:] = low
-        pair = jnp.concatenate([high, low], 0)
-        result = mul(lhs_out[...], pair)[:8]
-        put(raw, pl.ds(pl.multiple_of(8 * k, 8), 8), result + pltpu.roll(result, 4, 0))
-
-    def forward_some(i, carry):
-        for u in range(UNROLL):
-            forward(i * UNROLL + u)
-        return carry
-
-    lax.fori_loop(0, NZ // UNROLL, forward_some, 0)
+        feats[p][i] = features
+        value, up = activate(mul(lhs_in[...], features))
+        value1[p][i] = value
+        up1[p][i] = up
+        h1[p][i, :HID], h1[p][i, HID:] = split(value)
+
+    def layer_mid(i, p):
+        value, up = activate(two_halves(mul(lhs_mid[...], h1[p][i])))
+        value2[p][i] = value
+        up2[p][i] = up
+        h2[p][i, :HID], h2[p][i, HID:] = split(value)
+
+    def layer_out(i, p):
+        result = mul(lhs_out[...], h2[p][i])[:8]
+        row = pl.multiple_of(16 * i + 8 * p, 8)
+        put(raw, pl.ds(row, 8), result + pltpu.roll(result, 4, 0))
+
+    pipeline(layer_in, layer_mid, layer_out)
 
     def strided(ref, o):
         return get(ref, pl.ds(o, NZ, stride=8))
 
-    row = lax.broadcasted_iota(jnp.int32, (NZ, NZ), 0)
-    column = lax.broadcasted_iota(jnp.int32, (NZ, NZ), 1)
-    sign = 1 - 2 * facing
-    earlier = jnp.where((row - column) * sign > 0, 1.0, 0.0)
-    later = jnp.where((column - row) * sign > 0, 1.0, 0.0)
-
     def summed(mask, value):
-        mask = jnp.concatenate([mask] * 3, 1).astype(bf16)
         return mul(mask, jnp.concatenate(split3(value), 0).astype(bf16))
 
     raw_sigma = strided(raw, 0)
     optical = STEP_DEPTH * softplus(raw_sigma)
-    transmit = jnp.exp(-summed(earlier, optical))
+    transmit = jnp.exp(-summed(masks[:NZ], optical))
     weight = transmit * one_minus_exp(optical)
     gain = jnp.zeros_like(weight)
     for c in range(3):
@@ -225,10 +223,10 @@
         picture = jnp.sum(weight * rgb, 0, keepdims=True)
         for r in range(ROWS):
             image[c, r : r + 1, :] = picture[:, r * PY : (r + 1) * PY]
-        cot_c = jnp.concatenate([cot[c, r : r + 1, :] for r in range(ROWS)], 1)
+        cot_c = per_ray[c : c + 1, :]
         gain = gain + cot_c * rgb
         put(graw, pl.ds(c + 1, NZ, stride=8), weight * cot_c * (rgb * (1.0 - rgb)))
-    grad_optical = gain * transmit * jnp.exp(-optical) - summed(later, gain * weight)
+    grad_optical = gain * transmit * jnp.exp(-optical) - summed(masks[NZ:], gain * weight)
     put(graw, pl.ds(0, NZ, stride=8), STEP_DEPTH * grad_optical * logistic(raw_sigma))
 
     acc_mid[...] = jnp.zeros_like(acc_mid)
@@ -236,36 +234,54 @@
     acc_out[...] = jnp.zeros_like(acc_out)
     first = lax.broadcasted_iota(jnp.int32, (8, RAYS), 0) < 4
 
-    def backward(k):
-        g = get(graw, pl.ds(pl.multiple_of(8 * k, 8), 8))
+    def back_from_out(i, p):
+        g = get(graw, pl.ds(pl.multiple_of(16 * i + 8 * p, 8), 8))
         g = jnp.where(first, g, pltpu.roll(g, 4, 0))
         high = g.astype(bf16).astype(f32)
         pair = jnp.where(first, high, g - high)
         cotangent = jnp.concatenate([pair, jnp.where(first, high, 0.0)], 0).astype(bf16)
-        delta = mul(back_out[...], cotangent) * d2[k]
-        acc_out[...] += mul_t(cotangent, h2[k])
-        pair = jnp.concatenate(split(delta), 0)
-        acc_mid[...] += mul_t(h1[k], pair)
-        delta = two_halves(mul(back_mid[...], pair)) * d1[k]
-        pair = jnp.concatenate(split(delta), 0)
-        acc_in[...] += mul_t(feats[k], pair)
-
-    def backward_some(i, carry):
-        for u in range(UNROLL):
-            backward(i * UNROLL + u)
-        return carry
-
-    lax.fori_loop(0, NZ // UNROLL, backward_some, 0)
+        delta2[p][...] = mul(back_out[...], cotangent) * slope_of(value2[p][i], up2[p][i])
+        acc_out[...] += mul_t(cotangent, h2[p][i])
+
+    def back_from_mid(i, p):
+        pair = jnp.concatenate(split(delta2[p][...]), 0)
+        acc_mid[...] += mul_t(h1[p][i], pair)
+        delta1[p][...] = two_halves(mul(back_mid[...], pair)) * slope_of(value1[p][i], up1[p][i])
+
+    def back_from_in(i, p):
+        pair = jnp.concatenate(split(delta1[p][...]), 0)
+        acc_in[...] += mul_t(feats[p][i], pair)
+
+    pipeline(back_from_out, back_from_mid, back_from_in)
 
     grads[:HID] = two_sides(two_halves(acc_mid[...]))
     total = two_sides(acc_in[...])
     grads[HID : HID + CH] = total[:CH] + total[CH : 2 * CH]
-    for c in range(COND):
-        grads[HID + CH + c : HID + CH + c + 1] = cond[0, c] * total[3 * CH : 3 * CH + 1]
+    grads[HID + CH : HID + CH + COND] = per_channel[...] * total[3 * CH : 3 * CH + 1]
     total = two_sides(acc_out[...])[:8]
     used = HID + CH + COND
     grads[used : used + 8] = total + pltpu.roll(total, 4, 0)
     grads[used + 8 :] = jnp.zeros((grads.shape[0] - used - 8, HID), f32)
+
+
+def pipeline(first, second, third):
+    def step(i, carry):
+        third(i - 1, 0)
+        second(i - 1, 1)
+        first(i, 0)
+        third(i - 1, 1)
+        second(i, 0)
+        first(i, 1)
+        return carry
+
+    first(0, 0)
+    second(0, 0)
+    first(0, 1)
+    lax.fori_loop(1, NZ // 2, step, 0)
+    last = NZ // 2 - 1
+    third(last, 0)
+    second(last, 1)
+    third(last, 1)
 
 
 def sum_kernel(parts, out):
@@ -280,6 +296,10 @@
     grad_mid[...] = packed[:HID]
     grad_in[...] = packed[HID : HID + CH + COND]
     grad_out_t[...] = packed[HID + CH + COND : HID + CH + COND + 4]
+
+
+def room(mebibytes):
+    return pltpu.CompilerParams(vmem_limit_bytes=mebibytes * 2**20)
 
 
 def shape(dims, dtype=f32):
@@ -298,40 +318,54 @@
         out_specs=VMEM,
     )(offsets, shifts, volume.reshape(2 * CH * PX, PY))
     slices = exchange(rows, BRICK).reshape(NZ, ROWS, CH, PY)
-    weights = pl.pallas_call(
-        weights_kernel,
+    prepared = pl.pallas_call(
+        prepare_kernel,
         out_shape=(
+            shape((8, RAYS)),
+            shape((COND, HID)),
+            shape((2 * NZ, 3 * NZ), bf16),
             shape((HID, 32), bf16),
             shape((2 * HID, 2 * HID), bf16),
             shape((16, 2 * HID), bf16),
             shape((2 * HID, 2 * HID), bf16),
             shape((HID, 16), bf16),
         ),
-        in_specs=[SMEM, VMEM, VMEM, VMEM],
-        out_specs=(VMEM,) * 5,
-    )(cond, w_in, w_mid, w_out.T)
+        in_specs=[SMEM] * 3 + [VMEM] * 4,
+        out_specs=(VMEM,) * 8,
+        compiler_params=room(2),
+    )(offsets, order, cond, w_in, w_mid, w_out.T, cot_image[0])
+    half = NZ // 2
+    slabs = [
+        pltpu.VMEM((half, 32, RAYS), bf16),
+        pltpu.VMEM((half, 2 * HID, RAYS), bf16),
+        pltpu.VMEM((half, 2 * HID, RAYS), bf16),
+        *[pltpu.VMEM((half, HID, RAYS), f32)] * 4,
+    ]
     image, grads = pl.pallas_call(
         render_kernel,
         out_shape=(shape((3, ROWS, PY)), shape((PIECES * PIECE_ROWS, HID))),
-        in_specs=[SMEM, SMEM, SMEM] + [VMEM] * 7,
+        in_specs=[VMEM] * 9,
         out_specs=(VMEM, VMEM),
         scratch_shapes=[
-            pltpu.VMEM((NZ, 32, RAYS), bf16),
-            pltpu.VMEM((NZ, 2 * HID, RAYS), bf16),
-            pltpu.VMEM((NZ, HID, RAYS), f32),
-            pltpu.VMEM((NZ, 2 * HID, RAYS), bf16),
-            pltpu.VMEM((NZ, HID, RAYS), f32),
+            *slabs,
+            *slabs,
+            *[pltpu.VMEM((HID, RAYS), f32)] * 4,
             pltpu.VMEM((ROWS, NZ * 8, PY), f32),
             pltpu.VMEM((ROWS, NZ * 8, PY), f32),
             pltpu.VMEM((2 * HID, 2 * HID), f32),
             pltpu.VMEM((32, 2 * HID), f32),
             pltpu.VMEM((16, 2 * HID), f32),
         ],
-    )(offsets, order, cond, slices, cot_image[0], *weights)
+        compiler_params=room(34),
+    )(slices, *prepared)
 
     def total(parts):
         return pl.pallas_call(
-            sum_kernel, out_shape=shape(parts.shape), in_specs=[VMEM], out_specs=VMEM
+            sum_kernel,
+            out_shape=shape(parts.shape),
+            in_specs=[VMEM],
+            out_specs=VMEM,
+            compiler_params=room(2),
         )(parts)
 
     parts = grads.reshape(PIECES, PIECE_ROWS, HID)
@@ -343,6 +377,7 @@
         out_shape=(shape((CH + COND, HID)), shape((HID, HID)), shape((4, HID))),
         in_specs=[VMEM],
         out_specs=(VMEM,) * 3,
+        compiler_params=room(2),
     )(packed)
     return image[None], grad_in, grad_mid, grad_out_t.T
 

time: 85.3 us -> 69.7 us (0.82)
  Pallas kernels: 29.3 us -> 16.6 us
  blocking collectives: 42.6 us -> 39.6 us
    pallas_call x1, Pallas kernels: 21 us -> 13.1 us  [per_device(): pl.pallas_call(render_kernel, out_shape=(shape((3, ROWS, PY)), shape((PIE...]
    pallas_call x2, Pallas kernels: 3.16 us -> 0.05 us  [total(): pl.pallas_call(sum_kernel, out_shape=shape(parts.shape), in_specs=[VMEM],...]
    all_to_all x3, blocking collectives: 42.6 us -> 39.6 us  [exchange(): return lax.all_to_all(parts, axes, 0, 0, tiled=True)]
    pallas_call x1, Pallas kernels: 1.62 us -> 0.69 us  [per_device(): pl.pallas_call(prepare_kernel, out_shape=(shape((8, RAYS)), shape((COND,...]
    pallas_call x1, Pallas kernels: 1.54 us -> 0.64 us  [per_device(): pl.pallas_call(unpack_kernel, out_shape=(shape((CH + COND, HID)), shape((...]
  transfers between devices with their start and end apart: 1 -> 1, of which waited for: 1 -> 1; matrix products, arithmetic and copies ran while one was open for 0% -> 0% of each run, Pallas kernels for 2% -> 1%
where the time goes in v2:
time: 69.7 us; the launch traced here: 69.3 us
  blocking collectives  39.6 us (57%)
  Pallas kernels  16.6 us (24%)
  starting transfers between devices  6.65 us (10%)
  waiting for transfers between devices  4.46 us (6%)
  between operations  1.36 us (2%)
    all_to_all x3, blocking collectives, exchange(): return lax.all_to_all(parts, axes, 0, 0, tiled=True)  39.6 us
    pallas_call x1, Pallas kernels, per_device(): pl.pallas_call(render_kernel, out_shape=(shape((3, ROWS, PY)), shape((PIE...  13.1 us
    all_to_all x1, starting transfers between devices, exchange(): return lax.all_to_all(parts, axes, 0, 0, tiled=True)  6.65 us
    all_to_all x1, waiting for transfers between devices, exchange(): return lax.all_to_all(parts, axes, 0, 0, tiled=True)  4.46 us
    pallas_call x1, Pallas kernels, per_device(): pl.pallas_call(resample_kernel, out_shape=shape((8, 2, ROWS, CH, PY)), in...  2.03 us
  transfers between devices with their start and end apart: 1, of which 1 were waited for; matrix products, arithmetic and copies ran while one was open for 0% of the time, Pallas kernels for 1%

profile of v2, /device:TPU:1, one launch (start us, length us, event | category | flops | bytes accessed | tf_op | source)
XLA Modules:
  0.0 69.3 jit_solution(639443719935033008)
XLA Ops:
  0.6 2.0 %shard_map.120 = f32[8,2,4,8,128]{4,3,2,1,0:T(8,128)} custom-call(f32[1,3]{1,0:T(1,128)} %offsets.3, s32[1,2]{1,0:T(1,128)} %shifts.1, f32[512,128]{1,0:T(8,128)} %bitcast.13), custom_call_target="tpu_custom_call" | custom-call | tf_op jit(solution)/shard_map/pallas_call | solution.py:314
  2.7 0.0 copy-start
  2.7 0.0 copy-start.1
  2.7 0.0 copy-start.2
  2.7 6.7 %all-to-all-start = ((f32[8,2,4,8,128]{4,3,2,1,0:T(8,128)}), f32[8,2,4,8,128]{4,3,2,1,0:T(8,128)S(1)}, u32[]{:S(2)}, u32[]{:S(2)}) async-start(f32[8,2,4,8,128]{4,3,2,1,0:T(8,128)} %shard_map.120), calls=%async_computation | async-start | bytes 524288 | tf_op jit(solution)/shard_map/all_to_all | solution.py:310
  10.0 0.0 copy-start.3
  10.0 0.0 copy-start.4
  10.0 0.0 copy-start.5
  10.0 0.0 copy-done
  10.0 0.0 copy-done.1
  10.0 0.0 copy-done.2
  10.0 0.6 copy-done.3
  10.7 0.0 copy-done.4
  10.7 0.0 copy-done.5
  10.7 0.7 shard_map.121
  11.4 4.5 %all-to-all-done = f32[8,2,4,8,128]{4,3,2,1,0:T(8,128)S(1)} async-done(((f32[8,2,4,8,128]{4,3,2,1,0:T(8,128)}), f32[8,2,4,8,128]{4,3,2,1,0:T(8,128)S(1)}, u32[]{:S(2)}, u32[]{:S(2)}) %all-to-all-start) | async-done | bytes 262176 | tf_op jit(solution)/shard_map/all_to_all | solution.py:310
  15.8 13.1 %shard_map.122 = (f32[3,4,128]{2,1,0:T(4,128)}, f32[256,128]{1,0:T(8,128)S(1)}) custom-call(f32[16,4,8,128]{3,2,1,0:T(8,128)S(1)} %bitcast.8, f32[8,512]{1,0:T(8,128)S(1)} %get-tuple-element.17.per_ray, f32[8,128]{1,0:T(8,128)S(1)} %get-tuple-element.18.per_channel, bf16[32,48]{1,0:T(8,128)(2,1)S(1)} %get-tuple-element.19.masks, ...), custom_call_target="tpu_custom_call" | custom-call | tf_op jit(solution)/shard_map/pallas_call | solution.py:344
  29.0 9.6 %all_to_all.20.parts = f32[16,16,128]{2,1,0:T(8,128)S(1)} all-to-all(f32[16,16,128]{2,1,0:T(8,128)S(1)} %bitcast.10), channel_id=1, replica_groups=mesh['y_far'=2,'y_near'=2,'z'=8,'x'=4,'core'=2] {'y_near','x','core'}, dimensions={0} | all-to-all | bytes 262144 | tf_op jit(solution)/shard_map/all_to_all | solution.py:310
  38.6 19.4 %all_to_all.21.parts = f32[16,16,128]{2,1,0:T(8,128)S(1)} all-to-all(f32[16,16,128]{2,1,0:T(8,128)S(1)} %shard_map.123), channel_id=1, replica_groups=mesh['y_far'=2,'y_near'=2,'z'=8,'x'=4,'core'=2] {'y_far','z'}, dimensions={0} | all-to-all | bytes 262144 | tf_op jit(solution)/shard_map/all_to_all | solution.py:310
  58.0 10.7 %all_to_all.22 = f32[16,16,128]{2,1,0:T(8,128)S(1)} all-to-all(f32[16,16,128]{2,1,0:T(8,128)S(1)} %shard_map.124), channel_id=1, replica_groups=mesh['y_far'=2,'y_near'=2,'z'=8,'x'=4,'core'=2] {'y_near','x','core'}, dimensions={0} | all-to-all | bytes 262144 | tf_op jit(solution)/shard_map/all_to_all | solution.py:310
  68.7 0.6 shard_map.125
  (2 shorter events, 0.1 us)
Async XLA Ops:
  2.7 7.3 %copy-start = (f32[128,128]{1,0:T(8,128)S(1)}, f32[128,128]{1,0:T(8,128)}, u32[]{:S(2)}) copy-start(f32[128,128]{1,0:T(8,128)} %w_mid.1) | copy-start | bytes 196612
  2.7 7.4 %copy-start.1 = (f32[16,128]{1,0:T(8,128)S(1)}, f32[16,128]{1,0:T(8,128)}, u32[]{:S(2)}) copy-start(f32[16,128]{1,0:T(8,128)} %w_in.1) | copy-start | bytes 24580
  2.7 7.4 %copy-start.2 = (f32[1,3,4,128]{3,2,1,0:T(4,128)S(1)}, f32[1,3,4,128]{3,2,1,0:T(4,128)}, u32[]{:S(2)}) copy-start(f32[1,3,4,128]{3,2,1,0:T(4,128)} %param.17) | copy-start | bytes 18436
  2.7 13.1 %all-to-all-start = ((f32[8,2,4,8,128]{4,3,2,1,0:T(8,128)}), f32[8,2,4,8,128]{4,3,2,1,0:T(8,128)S(1)}, u32[]{:S(2)}, u32[]{:S(2)}) async-start(f32[8,2,4,8,128]{4,3,2,1,0:T(8,128)} %shard_map.120), calls=%async_computation | async-start | bytes 524288 | tf_op jit(solution)/shard_map/all_to_all | solution.py:310
  10.0 0.7 copy-start.3
  10.0 0.7 copy-start.4
  10.0 0.7 copy-start.5
